TPU v7x, 32 devices: a whole 2x2x4 slice. The times are simulated.
32 devices in a mesh: dp: 4 (over y, x), seg: 8 (over z, core).
Axes of the slice: x: 2, y: 2, z: 4, core: 2. Of those that a mesh axis runs over, the one named last changes fastest.
Arguments:
- inputs: bfloat16 [4, 4096, 768], P('dp', 'seg'), may hold values from -6 to 6
- doc_ids: int32 [4, 32], P('dp'), may hold values from 0 to 7, never falling along the last dimension, each value on 1 to 16 neighbouring positions
- cotangent: bfloat16 [4, 4096, 768], P('dp', 'seg'), may hold values from -6 to 6
- query_weight: bfloat16 [2, 768, 768], P(None, 'dp'), may hold values from -0.21875 to 0.21875
- query_bias: bfloat16 [2, 768], replicated, may hold values from -3 to 3
- key_weight: bfloat16 [2, 768, 768], P(None, 'dp'), may hold values from -0.21875 to 0.21875
- value_weight: bfloat16 [2, 768, 768], P(None, 'dp'), may hold values from -0.21875 to 0.21875
- value_bias: bfloat16 [2, 768], replicated, may hold values from -3 to 3
- out_weight: bfloat16 [2, 768, 768], P(None, 'dp'), may hold values from -1.75 to 1.75
- out_bias: bfloat16 [2, 768], replicated, may hold values from -3 to 3
- first_gain: bfloat16 [2, 768], replicated, may hold values from 0.5 to 1.5
- first_shift: bfloat16 [2, 768], replicated, may hold values from -2 to 2
- inner_weight: bfloat16 [2, 768, 3072], P(None, 'dp'), may hold values from -0.21875 to 0.21875
- inner_bias: bfloat16 [2, 3072], replicated, may hold values from -3 to 3
- outer_weight: bfloat16 [2, 3072, 768], P(None, 'dp'), may hold values from -0.109375 to 0.109375
- outer_bias: bfloat16 [2, 768], replicated, may hold values from -3 to 3
- second_gain: bfloat16 [2, 768], replicated, may hold values from 0.5 to 1.5
- second_shift: bfloat16 [2, 768], replicated, may hold values from -2 to 2
- segment_embed: bfloat16 [32, 768], replicated, may hold values from -3 to 3
Outputs:
- output: bfloat16 [4, 4096, 768], P('dp', 'seg')
- input_grad: bfloat16 [4, 4096, 768], P('dp', 'seg')
- grad_query_weight: float32 [2, 768, 768], P(None, 'dp')
- grad_query_bias: float32 [2, 768], P(None, 'dp')
- grad_key_weight: float32 [2, 768, 768], P(None, 'dp')
- grad_value_weight: float32 [2, 768, 768], P(None, 'dp')
- grad_value_bias: float32 [2, 768], P(None, 'dp')
- grad_out_weight: float32 [2, 768, 768], P(None, 'dp')
- grad_out_bias: float32 [2, 768], P(None, 'dp')
- grad_first_gain: float32 [2, 768], P(None, 'dp')
- grad_first_shift: float32 [2, 768], P(None, 'dp')
- grad_inner_weight: float32 [2, 768, 3072], P(None, 'dp')
- grad_inner_bias: float32 [2, 3072], P(None, 'dp')
- grad_outer_weight: float32 [2, 3072, 768], P(None, 'dp')
- grad_outer_bias: float32 [2, 768], P(None, 'dp')
- grad_second_gain: float32 [2, 768], P(None, 'dp')
- grad_second_shift: float32 [2, 768], P(None, 'dp')
- grad_segment_embed: float32 [32, 768], P(None, 'dp')
Inputs may be any that keep to these rules, and one draw needn't show every extreme that they name: `doc_ids`: along each row document numbers never fall; each document covers one to half of 32 consecutive segments, and some document of each row covers exactly half of 32.
All inputs are finite; a program needn't handle non-finite values.
Results may differ from a plain program's by a relative error of at most 0.02.
Values may be sent and summed in bfloat16 or wider, within the bound.
A program may use at most 256 MiB of HBM per device.

v0:
```python
import jax
import jax.numpy as jnp
from jax import lax
from jax.sharding import PartitionSpec as P

HEADS = 12
HEAD_DIM = 64
SEG_LEN = 128
epsilon = 1e-05


def normalize(values, gain, shift):
    centred = values - jnp.mean(values, axis=-1, keepdims=True)
    spread = jnp.mean(centred * centred, axis=-1, keepdims=True)
    return centred * lax.rsqrt(spread + epsilon) * gain + shift


def gelu_exact(values):
    return jax.nn.gelu(values, approximate=False)


def project(values, weight):
    return jnp.einsum("gnd,de->gne", values, weight, preferred_element_type=jnp.float32)


def back_project(values, weight):
    return jnp.einsum("gne,de->gnd", values, weight, preferred_element_type=jnp.float32)


def weight_grad(source, grads):
    return jnp.einsum("gnd,gne->de", source, grads, preferred_element_type=jnp.float32)


def row_total(values):
    return jnp.sum(values.astype(jnp.float32), axis=(0, 1))


def keep_pair(first_part, second_part):
    return (first_part, second_part)


def forward_layer(params, source, allowed, spread_keys):
    (
        query_weight,
        query_bias,
        key_weight,
        value_weight,
        value_bias,
        out_weight,
        out_bias,
        first_gain,
        first_shift,
        inner_weight,
        inner_bias,
        outer_weight,
        outer_bias,
        second_gain,
        second_shift,
    ) = params
    groups, length, width = source.shape
    queries = (project(source, query_weight) + query_bias.astype(jnp.float32)).astype(jnp.bfloat16)
    key_rows = project(source, key_weight).astype(jnp.bfloat16)
    value_rows = (project(source, value_weight) + value_bias.astype(jnp.float32)).astype(
        jnp.bfloat16
    )
    key_all, value_all = spread_keys(key_rows, value_rows)
    key_length = key_all.shape[1]
    query_heads = queries.reshape(groups, length, HEADS, HEAD_DIM)
    key_heads = key_all.reshape(groups, key_length, HEADS, HEAD_DIM)
    value_heads = value_all.reshape(groups, key_length, HEADS, HEAD_DIM)
    scores = (
        jnp.einsum("gqhe,gkhe->ghqk", query_heads, key_heads, preferred_element_type=jnp.float32)
        * 0.125
    )
    if allowed is not None:
        scores = jnp.where(allowed[:, None], scores, -1e30)
    attend = jax.nn.softmax(scores, axis=-1)
    attend_low = attend.astype(jnp.bfloat16)
    mixed = jnp.einsum(
        "ghqk,gkhe->gqhe", attend_low, value_heads, preferred_element_type=jnp.float32
    )
    mixed = mixed.astype(jnp.bfloat16).reshape(groups, length, width)
    branch = project(mixed, out_weight) + out_bias.astype(jnp.float32)
    hidden, first_pull = jax.vjp(
        normalize,
        source.astype(jnp.float32) + branch,
        first_gain.astype(jnp.float32),
        first_shift.astype(jnp.float32),
    )
    hidden_low = hidden.astype(jnp.bfloat16)
    inner = project(hidden_low, inner_weight) + inner_bias.astype(jnp.float32)
    active, gelu_pull = jax.vjp(gelu_exact, inner)
    active_low = active.astype(jnp.bfloat16)
    outer = project(active_low, outer_weight) + outer_bias.astype(jnp.float32)
    result, second_pull = jax.vjp(
        normalize, hidden + outer, second_gain.astype(jnp.float32), second_shift.astype(jnp.float32)
    )
    stored = (
        source,
        query_heads,
        key_heads,
        value_heads,
        attend,
        attend_low,
        mixed,
        first_pull,
        hidden_low,
        gelu_pull,
        active_low,
        second_pull,
    )
    return (result, stored)


def backward_layer(params, stored, grad_result, collect_keys):
    (
        query_weight,
        query_bias,
        key_weight,
        value_weight,
        value_bias,
        out_weight,
        out_bias,
        first_gain,
        first_shift,
        inner_weight,
        inner_bias,
        outer_weight,
        outer_bias,
        second_gain,
        second_shift,
    ) = params
    (
        source,
        query_heads,
        key_heads,
        value_heads,
        attend,
        attend_low,
        mixed,
        first_pull,
        hidden_low,
        gelu_pull,
        active_low,
        second_pull,
    ) = stored
    groups, length, width = source.shape
    key_length = key_heads.shape[1]
    grad_second_sum, grad_second_gain, grad_second_shift = second_pull(grad_result)
    grad_outer = grad_second_sum.astype(jnp.bfloat16)
    grad_outer_bias = row_total(grad_outer)
    grad_outer_weight = weight_grad(active_low, grad_outer)
    grad_active = back_project(grad_outer, outer_weight).astype(jnp.bfloat16)
    (grad_inner,) = gelu_pull(grad_active.astype(jnp.float32))
    grad_inner_low = grad_inner.astype(jnp.bfloat16)
    grad_inner_bias = row_total(grad_inner_low)
    grad_inner_weight = weight_grad(hidden_low, grad_inner_low)
    grad_hidden = grad_second_sum + back_project(grad_inner_low, inner_weight)
    grad_first_sum, grad_first_gain, grad_first_shift = first_pull(grad_hidden)
    grad_branch = grad_first_sum.astype(jnp.bfloat16)
    grad_out_bias = row_total(grad_branch)
    grad_out_weight = weight_grad(mixed, grad_branch)
    grad_mixed = back_project(grad_branch, out_weight).astype(jnp.bfloat16)
    grad_mixed = grad_mixed.reshape(groups, length, HEADS, HEAD_DIM)
    grad_attend = jnp.einsum(
        "gqhe,gkhe->ghqk", grad_mixed, value_heads, preferred_element_type=jnp.float32
    )
    grad_attend = grad_attend.astype(jnp.bfloat16).astype(jnp.float32)
    grad_value = jnp.einsum(
        "ghqk,gqhe->gkhe", attend_low, grad_mixed, preferred_element_type=jnp.float32
    )
    grad_value = grad_value.reshape(groups, key_length, width)
    grad_scores = attend * (grad_attend - jnp.sum(attend * grad_attend, axis=-1, keepdims=True))
    grad_scores = grad_scores.astype(jnp.bfloat16)
    grad_query = (
        jnp.einsum("ghqk,gkhe->gqhe", grad_scores, key_heads, preferred_element_type=jnp.float32)
        * 0.125
    )
    grad_query = grad_query.astype(jnp.bfloat16).reshape(groups, length, width)
    grad_key = (
        jnp.einsum("ghqk,gqhe->gkhe", grad_scores, query_heads, preferred_element_type=jnp.float32)
        * 0.125
    )
    grad_key = grad_key.reshape(groups, key_length, width)
    grad_key, grad_value = collect_keys(grad_key, grad_value)
    grad_key = grad_key.astype(jnp.bfloat16)
    grad_value = grad_value.astype(jnp.bfloat16)
    grad_source = (
        grad_first_sum
        + back_project(grad_query, query_weight)
        + back_project(grad_key, key_weight)
        + back_project(grad_value, value_weight)
    )
    gradients = (
        weight_grad(source, grad_query),
        row_total(grad_query),
        weight_grad(source, grad_key),
        weight_grad(source, grad_value),
        row_total(grad_value),
        grad_out_weight,
        grad_out_bias,
        grad_first_gain,
        grad_first_shift,
        grad_inner_weight,
        grad_inner_bias,
        grad_outer_weight,
        grad_outer_bias,
        grad_second_gain,
        grad_second_shift,
    )
    return (grad_source, gradients)


def shards(
    inputs,
    doc_ids,
    cotangent,
    query_weight,
    query_bias,
    key_weight,
    value_weight,
    value_bias,
    out_weight,
    out_bias,
    first_gain,
    first_shift,
    inner_weight,
    inner_bias,
    outer_weight,
    outer_bias,
    second_gain,
    second_shift,
    segment_embed,
):
    seg_count = lax.axis_size("seg")
    seg_index = lax.axis_index("seg")
    group_rows, local_length, width = inputs.shape
    seg_local = local_length // SEG_LEN
    query_full, key_full, value_full, out_full, inner_full, outer_full = (
        lax.all_gather(query_weight, "dp", axis=1, tiled=True),
        lax.all_gather(key_weight, "dp", axis=1, tiled=True),
        lax.all_gather(value_weight, "dp", axis=1, tiled=True),
        lax.all_gather(out_weight, "dp", axis=1, tiled=True),
        lax.all_gather(inner_weight, "dp", axis=1, tiled=True),
        lax.all_gather(outer_weight, "dp", axis=1, tiled=True),
    )
    stacked = (
        query_full,
        query_bias,
        key_full,
        value_full,
        value_bias,
        out_full,
        out_bias,
        first_gain,
        first_shift,
        inner_full,
        inner_bias,
        outer_full,
        outer_bias,
        second_gain,
        second_shift,
    )
    first_params = tuple((weight[0] for weight in stacked))
    cross_params = tuple((weight[1] for weight in stacked))
    pieces = inputs.reshape(group_rows * seg_local, SEG_LEN, width)
    segment_out, segment_stored = forward_layer(first_params, pieces, None, keep_pair)
    segment_grid = segment_out.reshape(group_rows, seg_local, SEG_LEN, width)
    position = lax.dynamic_slice_in_dim(segment_embed, seg_index * seg_local, seg_local, 0).astype(
        jnp.float32
    )
    heads_in = (segment_grid[:, :, 0, :] + position).astype(jnp.bfloat16)
    row_input = lax.all_gather(heads_in, "seg", axis=1, tiled=True)
    allowed = doc_ids[:, :, None] == doc_ids[:, None, :]
    cross_out, cross_stored = forward_layer(cross_params, row_input, allowed, keep_pair)
    returned = lax.dynamic_slice_in_dim(cross_out, seg_index * seg_local, seg_local, 1).astype(
        jnp.bfloat16
    )
    output = jnp.concatenate(
        [returned[:, :, None, :], segment_grid[:, :, 1:, :].astype(jnp.bfloat16)], axis=2
    )
    output = output.reshape(group_rows, local_length, width)
    cot_grid = cotangent.reshape(group_rows, seg_local, SEG_LEN, width)
    cot_heads = cot_grid[:, :, 0, :]
    grad_cross = lax.all_gather(cot_heads, "seg", axis=1, tiled=True)
    grad_row_input, cross_grads = backward_layer(
        cross_params, cross_stored, grad_cross.astype(jnp.float32), keep_pair
    )
    grad_row_low = grad_row_input.astype(jnp.bfloat16)
    factor = 1.0 / seg_count
    embed_grad = jnp.sum(grad_row_low.astype(jnp.float32), axis=0) * factor
    cross_grads = tuple((part * factor for part in cross_grads))
    grad_heads = lax.dynamic_slice_in_dim(grad_row_low, seg_index * seg_local, seg_local, 1)
    grad_grid = jnp.concatenate(
        [grad_heads[:, :, None, :].astype(jnp.float32), cot_grid[:, :, 1:, :].astype(jnp.float32)],
        axis=2,
    )
    grad_grid = grad_grid.reshape(group_rows * seg_local, SEG_LEN, width)
    grad_pieces, segment_grads = backward_layer(first_params, segment_stored, grad_grid, keep_pair)
    input_grad = grad_pieces.astype(jnp.bfloat16).reshape(group_rows, local_length, width)
    shares = (
        lax.psum_scatter(segment_grads[0], "dp", scatter_dimension=0, tiled=True),
        lax.psum_scatter(segment_grads[1], "dp", scatter_dimension=0, tiled=True),
        lax.psum_scatter(segment_grads[2], "dp", scatter_dimension=0, tiled=True),
        lax.psum_scatter(segment_grads[3], "dp", scatter_dimension=0, tiled=True),
        lax.psum_scatter(segment_grads[4], "dp", scatter_dimension=0, tiled=True),
        lax.psum_scatter(segment_grads[5], "dp", scatter_dimension=0, tiled=True),
        lax.psum_scatter(segment_grads[6], "dp", scatter_dimension=0, tiled=True),
        lax.psum_scatter(segment_grads[7], "dp", scatter_dimension=0, tiled=True),
        lax.psum_scatter(segment_grads[8], "dp", scatter_dimension=0, tiled=True),
        lax.psum_scatter(segment_grads[9], "dp", scatter_dimension=0, tiled=True),
        lax.psum_scatter(segment_grads[10], "dp", scatter_dimension=0, tiled=True),
        lax.psum_scatter(segment_grads[11], "dp", scatter_dimension=0, tiled=True),
        lax.psum_scatter(segment_grads[12], "dp", scatter_dimension=0, tiled=True),
        lax.psum_scatter(segment_grads[13], "dp", scatter_dimension=0, tiled=True),
        lax.psum_scatter(segment_grads[14], "dp", scatter_dimension=0, tiled=True),
        lax.psum_scatter(cross_grads[0], "dp", scatter_dimension=0, tiled=True),
        lax.psum_scatter(cross_grads[1], "dp", scatter_dimension=0, tiled=True),
        lax.psum_scatter(cross_grads[2], "dp", scatter_dimension=0, tiled=True),
        lax.psum_scatter(cross_grads[3], "dp", scatter_dimension=0, tiled=True),
        lax.psum_scatter(cross_grads[4], "dp", scatter_dimension=0, tiled=True),
        lax.psum_scatter(cross_grads[5], "dp", scatter_dimension=0, tiled=True),
        lax.psum_scatter(cross_grads[6], "dp", scatter_dimension=0, tiled=True),
        lax.psum_scatter(cross_grads[7], "dp", scatter_dimension=0, tiled=True),
        lax.psum_scatter(cross_grads[8], "dp", scatter_dimension=0, tiled=True),
        lax.psum_scatter(cross_grads[9], "dp", scatter_dimension=0, tiled=True),
        lax.psum_scatter(cross_grads[10], "dp", scatter_dimension=0, tiled=True),
        lax.psum_scatter(cross_grads[11], "dp", scatter_dimension=0, tiled=True),
        lax.psum_scatter(cross_grads[12], "dp", scatter_dimension=0, tiled=True),
        lax.psum_scatter(cross_grads[13], "dp", scatter_dimension=0, tiled=True),
        lax.psum_scatter(cross_grads[14], "dp", scatter_dimension=0, tiled=True),
        lax.psum_scatter(embed_grad, "dp", scatter_dimension=1, tiled=True),
    )
    summed = lax.psum(
        (
            shares[0],
            shares[1],
            shares[2],
            shares[3],
            shares[4],
            shares[5],
            shares[6],
            shares[7],
            shares[8],
            shares[9],
            shares[10],
            shares[11],
            shares[12],
            shares[13],
            shares[14],
            shares[15],
            shares[16],
            shares[17],
            shares[18],
            shares[19],
            shares[20],
            shares[21],
            shares[22],
            shares[23],
            shares[24],
            shares[25],
            shares[26],
            shares[27],
            shares[28],
            shares[29],
            shares[30],
        ),
        "seg",
    )
    totals = tuple((jnp.stack([summed[index], summed[index + 15]]) for index in range(15)))
    totals = totals + (summed[30],)
    return (output, input_grad) + tuple(totals)


def solution(mesh):
    placed = (
        P("dp", "seg", None),
        P("dp", None),
        P("dp", "seg", None),
        P(None, "dp", None),
        P(),
        P(None, "dp", None),
        P(None, "dp", None),
        P(),
        P(None, "dp", None),
        P(),
        P(),
        P(),
        P(None, "dp", None),
        P(),
        P(None, "dp", None),
        P(),
        P(),
        P(),
        P(),
    )
    return jax.shard_map(
        shards,
        mesh=mesh,
        in_specs=placed,
        out_specs=(
            P("dp", "seg", None),
            P("dp", "seg", None),
            P(None, "dp", None),
            P(None, "dp"),
            P(None, "dp", None),
            P(None, "dp", None),
            P(None, "dp"),
            P(None, "dp", None),
            P(None, "dp"),
            P(None, "dp"),
            P(None, "dp"),
            P(None, "dp", None),
            P(None, "dp"),
            P(None, "dp", None),
            P(None, "dp"),
            P(None, "dp"),
            P(None, "dp"),
            P(None, "dp"),
        ),
        check_vma=False,
    )
```

profile of v0, /device:TPU:0, one launch (start us, length us, event | category | flops | bytes accessed | tf_op | source)
XLA Modules:
  0.0 1615.4 jit_solution(5747079479511893777)
XLA Ops:
  11.4 15.6 all-gather.1
  32.1 17.8 %all-gather.10.cloned.1.call-done = bf16[2,768,768]{2,1,0:T(8,128)(2,1)} async-done(((bf16[2,192,768]{2,1,0:T(8,128)(2,1)}), bf16[2,768,768]{2,1,0:T(8,128)(2,1)}) %all-gather.10.cloned.1.call-update) | async-done | bytes 2359312 | tf_op jit(solution)/shard_map/all_gather | solution.py:242
  53.2 36.0 %all-gather.12.cloned.1.call-done = bf16[2,768,768]{2,1,0:T(8,128)(2,1)} async-done(((bf16[2,192,768]{2,1,0:T(8,128)(2,1)}), bf16[2,768,768]{2,1,0:T(8,128)(2,1)}) %all-gather.12.cloned.1.call-update) | async-done | bytes 2359312 | tf_op jit(solution)/shard_map/all_gather | solution.py:240
  91.6 36.8 %all-gather.14.cloned.1.call-done = bf16[2,768,768]{2,1,0:T(8,128)(2,1)} async-done(((bf16[2,192,768]{2,1,0:T(8,128)(2,1)}), bf16[2,768,768]{2,1,0:T(8,128)(2,1)}) %all-gather.14.cloned.1.call-update) | async-done | bytes 2359312 | tf_op jit(solution)/shard_map/all_gather | solution.py:241
  130.8 2.9 fusion.106
  133.8 2.7 convolution_convert_fusion.5
  136.5 31.0 %all-gather.16.cloned.1.call-done = bf16[2,768,768]{2,1,0:T(8,128)(2,1)} async-done(((bf16[2,192,768]{2,1,0:T(8,128)(2,1)}), bf16[2,768,768]{2,1,0:T(8,128)(2,1)}) %all-gather.16.cloned.1.call-update) | async-done | bytes 2359312 | tf_op jit(solution)/shard_map/all_gather | solution.py:243
  170.0 95.4 %all-gather.18.cloned.1.call-done = bf16[2,768,3072]{2,1,0:T(8,128)(2,1)} async-done(((bf16[2,192,3072]{2,1,0:T(8,128)(2,1)}), bf16[2,768,3072]{2,1,0:T(8,128)(2,1)}) %all-gather.18.cloned.1.call-update) | async-done | bytes 9437200 | tf_op jit(solution)/shard_map/all_gather | solution.py:244
  265.4 6.9 fusion.33
  272.3 3.3 copy-done.7
  275.6 15.7 multiply_convert_fusion
  291.3 72.1 %all-gather.20.cloned.1.call-done = bf16[2,3072,768]{2,1,0:T(8,128)(2,1)} async-done(((bf16[2,768,768]{2,1,0:T(8,128)(2,1)}), bf16[2,3072,768]{2,1,0:T(8,128)(2,1)}) %all-gather.20.cloned.1.call-update) | async-done | bytes 9437200 | tf_op jit(solution)/shard_map/all_gather | solution.py:245
  363.3 6.0 fusion.108
  372.5 14.1 all-gather.2
  400.7 3.4 fusion.22
  404.2 4.5 fusion.46
  423.3 2.4 convert_reduce_fusion.6
  439.2 9.9 multiply_reduce_fusion.1
  450.6 8.9 convert_reduce_fusion
  459.6 3.6 multiply_reduce_fusion.2
  467.9 3.2 convert_reduce_fusion.3
  474.2 3.1 copy.176
  478.4 2.9 fusion.25
  486.1 3.0 copy.168
  489.5 2.4 multiply_convert_fusion.1
  494.9 3.1 copy.172
  501.7 2.8 convolution_multiply_fusion.2
  510.6 7.2 convolution_bitcast_fusion.1
  519.8 6.2 convolution_bitcast_fusion
  527.0 5.9 convolution_multiply_fusion
  533.8 5.0 convolution_multiply_fusion.1
  552.0 3.3 reduce-scatter.40.cloned.1.call-done
  557.5 38.3 %reduce-scatter.44.cloned.1.call-done = f32[192,768]{1,0:T(8,128)} async-done(((f32[768,768]{1,0:T(8,128)}), f32[192,768]{1,0:T(8,128)}) %reduce-scatter.44.cloned.1.call-update) | async-done | bytes 589840
  598.0 38.1 %reduce-scatter.52.cloned.1.call-done = f32[192,768]{1,0:T(8,128)} async-done(((f32[768,768]{1,0:T(8,128)}), f32[192,768]{1,0:T(8,128)}) %reduce-scatter.52.cloned.1.call-update) | async-done | bytes 589840
  638.3 38.2 %reduce-scatter.54.cloned.1.call-done = f32[192,768]{1,0:T(8,128)} async-done(((f32[768,768]{1,0:T(8,128)}), f32[192,768]{1,0:T(8,128)}) %reduce-scatter.54.cloned.1.call-update) | async-done | bytes 589840
  678.8 38.1 %reduce-scatter.50.cloned.1.call-done = f32[192,768]{1,0:T(8,128)} async-done(((f32[768,768]{1,0:T(8,128)}), f32[192,768]{1,0:T(8,128)}) %reduce-scatter.50.cloned.1.call-update) | async-done | bytes 589840
  719.1 38.8 %reduce-scatter.42.cloned.1.call-done = f32[192,768]{1,0:T(8,128)} async-done(((f32[768,768]{1,0:T(8,128)}), f32[192,768]{1,0:T(8,128)}) %reduce-scatter.42.cloned.1.call-update) | async-done | bytes 589840
  760.1 38.1 %reduce-scatter.46.cloned.1.call-done = f32[192,768]{1,0:T(8,128)} async-done(((f32[768,768]{1,0:T(8,128)}), f32[192,768]{1,0:T(8,128)}) %reduce-scatter.46.cloned.1.call-update) | async-done | bytes 589840
  800.4 95.7 %reduce-scatter.32.cloned.1.call-done = f32[192,3072]{1,0:T(8,128)} async-done(((f32[768,3072]{1,0:T(8,128)}), f32[192,3072]{1,0:T(8,128)}) %reduce-scatter.32.cloned.1.call-update) | async-done | bytes 2359312 | tf_op jit(solution)/shard_map/reduce_scatter | solution.py:311
  896.1 97.9 %reduce-scatter.36.cloned.1.call-done = f32[768,768]{1,0:T(8,128)} async-done(((f32[3072,768]{1,0:T(8,128)}), f32[768,768]{1,0:T(8,128)}) %reduce-scatter.36.cloned.1.call-update) | async-done | bytes 2359312 | tf_op jit(solution)/shard_map/reduce_scatter | solution.py:313
  994.0 97.9 %reduce-scatter.38.cloned.1.call-done = f32[768,768]{1,0:T(8,128)} async-done(((f32[3072,768]{1,0:T(8,128)}), f32[768,768]{1,0:T(8,128)}) %reduce-scatter.38.cloned.1.call-update) | async-done | bytes 2359312 | tf_op jit(solution)/shard_map/reduce_scatter | solution.py:328
  1091.9 97.9 %reduce-scatter.34.cloned.1.call-done = f32[192,3072]{1,0:T(8,128)} async-done(((f32[768,3072]{1,0:T(8,128)}), f32[192,3072]{1,0:T(8,128)}) %reduce-scatter.34.cloned.1.call-update) | async-done | bytes 2359312 | tf_op jit(solution)/shard_map/reduce_scatter | solution.py:326
  1200.1 44.1 %all-reduce.26.cloned.1.call-done = (f32[768]{0:T(1024)}, f32[768]{0:T(1024)}, f32[768]{0:T(1024)}, f32[768]{0:T(1024)}, f32[768]{0:T(1024)}, /*index=5*/f32[768...) async-done(((f32[768]{0:T(1024)}, f32[768]{0:T(1024)}, ...) | async-done | bytes 73744
  1257.8 13.8 reduce-scatter.56.cloned.1.call-done
  1272.6 30.8 %all-reduce.18 = (f32[1,192]{1,0:T(1,128)S(1)}, f32[1,192]{1,0:T(1,128)S(1)}, f32[1,192]{1,0:T(1,128)S(1)}, f32[1,192]{1,0:T(1,128)S(1)}, f32[1,192]{1,0:T(1,128...) all-reduce(f32[1,192]{1,0:T(1,128)S(1)} %bitcast.354, ...), channel_id=1, replica_groups=mesh['dp'=4,'seg'=8] {'seg'}, use_global_device_ids=true, to_apply=%region_31.32 | all-reduce | flops 10752 | bytes 86016 | tf_op jit(solution)/shard_map/psum | solution.py:334
  1308.7 282.4 %all-reduce.24.cloned.1.call-done = (f32[1,192,768]{1,2,0:T(8,128)}, f32[1,192,768]{1,2,0:T(8,128)}, f32[1,192,768]{1,2,0:T(8,128)}, f32[1,192,768]{1,2,0:T(8,12...) async-done(((f32[1,192,768]{1,2,0:T(8,128)}, ...) | async-done | bytes 14155792 | tf_op jit(solution)/shard_map/psum | solution.py:334
  1600.4 5.2 pad_maximum_fusion
  1605.6 2.5 pad_maximum_fusion.1
  (434 shorter events, 163.0 us)
Async XLA Ops:
  7.2 42.8 %all-gather.10.cloned.1.call-start = ((), (), s32[]{:S(2)}) async-start(), calls=%async_computation.13 | async-start | bytes 2949120 | tf_op jit(solution)/shard_map/all_gather | solution.py:242
  7.9 81.2 %all-gather.12.cloned.1.call-start = ((), (), s32[]{:S(2)}) async-start(), calls=%async_computation.14 | async-start | bytes 2949120 | tf_op jit(solution)/shard_map/all_gather | solution.py:240
  8.7 119.7 %all-gather.14.cloned.1.call-start = ((), (), s32[]{:S(2)}) async-start(), calls=%async_computation.15 | async-start | bytes 2949120 | tf_op jit(solution)/shard_map/all_gather | solution.py:241
  9.4 158.0 %all-gather.16.cloned.1.call-start = ((), (), s32[]{:S(2)}) async-start(), calls=%async_computation.16 | async-start | bytes 2949120 | tf_op jit(solution)/shard_map/all_gather | solution.py:243
  10.0 17.0 %copy-start.83 = (bf16[2,768]{1,0:T(2,128)(2,1)S(1)}, bf16[2,768]{1,0:T(2,128)(2,1)}, u32[]{:S(2)}) copy-start(bf16[2,768]{1,0:T(2,128)(2,1)} %param.23) | copy-start | bytes 9220
  10.0 17.0 %copy-start.84 = (bf16[2,768]{1,0:T(2,128)(2,1)S(1)}, bf16[2,768]{1,0:T(2,128)(2,1)}, u32[]{:S(2)}) copy-start(bf16[2,768]{1,0:T(2,128)(2,1)} %param.26) | copy-start | bytes 9220
  10.0 17.0 %copy-start.85 = (bf16[2,768]{1,0:T(2,128)(2,1)S(1)}, bf16[2,768]{1,0:T(2,128)(2,1)}, u32[]{:S(2)}) copy-start(bf16[2,768]{1,0:T(2,128)(2,1)} %param.28) | copy-start | bytes 9220
  10.0 17.6 %copy-start.86 = (bf16[2,768]{1,0:T(2,128)(2,1)S(1)}, bf16[2,768]{1,0:T(2,128)(2,1)}, u32[]{:S(2)}) copy-start(bf16[2,768]{1,0:T(2,128)(2,1)} %param.29) | copy-start | bytes 9220
  10.0 18.2 %copy-start.87 = (bf16[2,768]{1,0:T(2,128)(2,1)S(1)}, bf16[2,768]{1,0:T(2,128)(2,1)}, u32[]{:S(2)}) copy-start(bf16[2,768]{1,0:T(2,128)(2,1)} %param.34) | copy-start | bytes 9220
  10.1 18.2 %copy-start.88 = (bf16[2,768]{1,0:T(2,128)(2,1)S(1)}, bf16[2,768]{1,0:T(2,128)(2,1)}, u32[]{:S(2)}) copy-start(bf16[2,768]{1,0:T(2,128)(2,1)} %param.30) | copy-start | bytes 9220
  10.1 18.8 %copy-start.89 = (bf16[2,768]{1,0:T(2,128)(2,1)S(1)}, bf16[2,768]{1,0:T(2,128)(2,1)}, u32[]{:S(2)}) copy-start(bf16[2,768]{1,0:T(2,128)(2,1)} %param.36) | copy-start | bytes 9220
  10.1 18.8 %copy-start.90 = (bf16[2,768]{1,0:T(2,128)(2,1)S(1)}, bf16[2,768]{1,0:T(2,128)(2,1)}, u32[]{:S(2)}) copy-start(bf16[2,768]{1,0:T(2,128)(2,1)} %param.35) | copy-start | bytes 9220
  10.1 19.5 %copy-start.99 = (s32[1,32]{1,0:T(1,128)S(1)}, s32[1,32]{1,0:T(1,128)}, u32[]{:S(2)}) copy-start(s32[1,32]{1,0:T(1,128)} %param.20) | copy-start | bytes 388
  10.1 255.3 %all-gather.18.cloned.1.call-start = ((), (), s32[]{:S(2)}) async-start(), calls=%async_computation.17 | async-start | bytes 11796480 | tf_op jit(solution)/shard_map/all_gather | solution.py:244
  10.7 20.8 %copy-start.66 = (bf16[2,3072]{1,0:T(2,128)(2,1)S(1)}, bf16[2,3072]{1,0:T(2,128)(2,1)}, u32[]{:S(2)}) copy-start(bf16[2,3072]{1,0:T(2,128)(2,1)} %param.32) | copy-start | bytes 36868
  10.7 39.3 %copy-start.3 = (bf16[1,512,768]{2,1,0:T(8,128)(2,1)S(1)}, bf16[1,512,768]{2,1,0:T(8,128)(2,1)}, u32[]{:S(2)}) copy-start(bf16[1,512,768]{2,1,0:T(8,128)(2,1)} %param.19) | copy-start | bytes 2359300
  10.7 352.6 %all-gather.20.cloned.1.call-start = ((), (), s32[]{:S(2)}) async-start(), calls=%async_computation.18 | async-start | bytes 11796480 | tf_op jit(solution)/shard_map/all_gather | solution.py:245
  11.3 538.5 %reduce-scatter.48.cloned.1.call-start = ((), (), s32[]{:S(2)}) async-start(), calls=%async_computation.27 | async-start | bytes 2949120
  28.3 335.1 %copy-start.81 = (f32[768]{0:T(1024)}, f32[768]{0:T(1024)S(1)}, u32[]{:S(2)}) copy-start(f32[768]{0:T(1024)S(1)} %get-tuple-element.91) | copy-start | bytes 9220
  28.9 334.4 %copy-start.96 = (f32[768]{0:T(1024)}, f32[768]{0:T(1024)S(1)}, u32[]{:S(2)}) copy-start(f32[768]{0:T(1024)S(1)} %get-tuple-element.207) | copy-start | bytes 9220
  29.5 340.7 %copy-start.58 = (f32[768]{0:T(1024)}, f32[768]{0:T(1024)S(1)}, u32[]{:S(2)}) copy-start(f32[768]{0:T(1024)S(1)} %get-tuple-element.209) | copy-start | bytes 9220
  32.1 240.2 %copy-start.64 = (f32[1,3072]{1,0:T(1,128)}, f32[1,3072]{1,0:T(1,128)S(1)}, u32[]{:S(2)}) copy-start(f32[1,3072]{1,0:T(1,128)S(1)} %get-tuple-element.178) | copy-start | bytes 36868
  91.6 39.2 %copy-start.14 = (bf16[4,128,768]{1,2,0:T(8,128)(2,1)}, bf16[4,128,768]{1,2,0:T(8,128)(2,1)S(1)}, u32[]{:S(2)}) copy-start(bf16[4,128,768]{1,2,0:T(8,128)(2,1)S(1)} %copy.115) | copy-start | bytes 2359300
  136.5 33.5 %copy-start.17 = (bf16[4,12,64,128]{3,2,1,0:T(8,128)(2,1)}, bf16[4,12,64,128]{3,2,1,0:T(8,128)(2,1)S(1)}, u32[]{:S(2)}) copy-start(bf16[4,12,64,128]{3,2,1,0:T(8,128)(2,1)S(1)} %convolution_convert_fusion.5) | copy-start | bytes 2359300
  169.7 193.7 %copy-start.71 = (f32[4,128]{1,0:T(4,128)}, f32[4,128]{1,0:T(4,128)S(1)}, u32[]{:S(2)}) copy-start(f32[4,128]{1,0:T(4,128)S(1)} %broadcast_multiply_fusion.11) | copy-start | bytes 6148
  170.0 95.4 %copy-start.73 = (f32[4,128]{1,0:T(4,128)}, f32[4,128]{1,0:T(4,128)S(1)}, u32[]{:S(2)}) copy-start(f32[4,128]{1,0:T(4,128)S(1)} %multiply_reduce_fusion.6) | copy-start | bytes 6148
  170.0 193.3 %copy-start.93 = (f32[4,128]{1,0:T(4,128)}, f32[4,128]{1,0:T(4,128)S(1)}, u32[]{:S(2)}) copy-start(f32[4,128]{1,0:T(4,128)S(1)} %fusion.95) | copy-start | bytes 6148
  400.7 11.4 copy-start.101
  404.2 10.3 slice-start.2
  404.2 10.3 slice-start.3
  417.8 9.9 copy-start.100
  431.9 18.7 %slice-start = ((s8[6291456]{0:T(1024)(128)(4,1)}), s8[4194304]{0:T(1024)(128)(4,1)S(1)}, s32[]{:S(2)}) async-start(s8[6291456]{0:T(1024)(128)(4,1)} %bitcast.309), calls=%async_computation.34 | async-start | bytes 8388608
  435.7 13.3 copy-start.76
  439.2 11.4 slice-start.1
  477.3 78.0 %reduce-scatter.40.cloned.1.call-start = ((), (), s32[]{:S(2)}) async-start(), calls=%async_computation.23 | async-start | bytes 2949120
  489.2 106.6 %reduce-scatter.44.cloned.1.call-start = ((), (), s32[]{:S(2)}) async-start(), calls=%async_computation.25 | async-start | bytes 2949120
  498.1 138.0 %reduce-scatter.52.cloned.1.call-start = ((), (), s32[]{:S(2)}) async-start(), calls=%async_computation.29 | async-start | bytes 2949120
  501.7 174.9 %reduce-scatter.54.cloned.1.call-start = ((), (), s32[]{:S(2)}) async-start(), calls=%async_computation.30 | async-start | bytes 2949120
  504.6 212.3 %reduce-scatter.50.cloned.1.call-start = ((), (), s32[]{:S(2)}) async-start(), calls=%async_computation.28 | async-start | bytes 2949120
  506.6 251.3 %reduce-scatter.42.cloned.1.call-start = ((), (), s32[]{:S(2)}) async-start(), calls=%async_computation.24 | async-start | bytes 2949120
  508.6 289.6 %reduce-scatter.46.cloned.1.call-start = ((), (), s32[]{:S(2)}) async-start(), calls=%async_computation.26 | async-start | bytes 2949120
  510.6 385.5 %reduce-scatter.32.cloned.1.call-start = ((), (), s32[]{:S(2)}) async-start(), calls=%async_computation.19 | async-start | bytes 11796480 | tf_op jit(solution)/shard_map/reduce_scatter | solution.py:311
  517.9 476.1 %reduce-scatter.36.cloned.1.call-start = ((), (), s32[]{:S(2)}) async-start(), calls=%async_computation.21 | async-start | bytes 11796480 | tf_op jit(solution)/shard_map/reduce_scatter | solution.py:313
  526.0 565.9 %reduce-scatter.38.cloned.1.call-start = ((), (), s32[]{:S(2)}) async-start(), calls=%async_computation.22 | async-start | bytes 11796480 | tf_op jit(solution)/shard_map/reduce_scatter | solution.py:328
  532.9 656.9 %reduce-scatter.34.cloned.1.call-start = ((), (), s32[]{:S(2)}) async-start(), calls=%async_computation.20 | async-start | bytes 11796480 | tf_op jit(solution)/shard_map/reduce_scatter | solution.py:326
  538.9 705.3 %all-reduce.26.cloned.1.call-start = ((), (), s32[]{:S(2)}) async-start(), calls=%async_computation.33 | async-start | bytes 180224
  548.4 723.2 %reduce-scatter.56.cloned.1.call-start = ((), (), s32[]{:S(2)}) async-start(), calls=%async_computation.31 | async-start | bytes 491520
  549.5 1041.6 %all-reduce.24.cloned.1.call-start = ((), (), s32[]{:S(2)}) async-start(), calls=%async_computation.32 | async-start | bytes 31457280 | tf_op jit(solution)/shard_map/psum | solution.py:334
  (85 other events, 315.0 us)
Sparse Core Ops, SparseCore 0:
  9.8 40.0 all-gather.9
  51.8 37.3 all-gather.11
  91.0 37.3 all-gather.13
  130.1 37.3 all-gather.15
  169.1 96.1 all-gather.17
  267.1 96.1 all-gather.19
  477.4 37.3 reduce-scatter.47
  517.9 37.3 reduce-scatter.39
  558.3 37.3 reduce-scatter.43
  598.6 37.3 reduce-scatter.51
  639.1 37.3 reduce-scatter.53
  679.4 37.3 reduce-scatter.49
  720.5 37.3 reduce-scatter.41
  760.8 37.3 reduce-scatter.45
  801.2 94.8 reduce-scatter.31
  899.1 94.8 reduce-scatter.35
  997.0 94.8 reduce-scatter.37
  1094.8 94.8 reduce-scatter.33
  1195.7 48.4 all-reduce.25
  1246.9 24.6 reduce-scatter.55
  1276.2 314.8 all-reduce.23
where the time goes:
time: 1630 us; the launch traced here: 1620 us
  waiting for transfers between devices  1260 us (77%)
  matrix products  130 us (8%)
  local copies, waits for them, and re-layouts  81.8 us (5%)
  other arithmetic  69.1 us (4%)
  blocking collectives  60.5 us (4%)
  between operations  17.4 us (1%)
    unnamed x31, waiting for transfers between devices  295 us
    psum x1, waiting for transfers between devices, shards(): lax.psum((shares[0], shares[1], shares[2], shares[3], shares[4], shares[5...  282 us
    reduce_scatter x1, waiting for transfers between devices, shards(): lax.psum_scatter(cross_grads[9], 'dp', scatter_dimension=0, tiled=True)  97.9 us
    reduce_scatter x1, waiting for transfers between devices, shards(): lax.psum_scatter(segment_grads[11], 'dp', scatter_dimension=0, tiled=True)  97.9 us
    reduce_scatter x1, waiting for transfers between devices, shards(): lax.psum_scatter(cross_grads[11], 'dp', scatter_dimension=0, tiled=True)  97.9 us
    reduce_scatter x1, waiting for transfers between devices, shards(): lax.psum_scatter(segment_grads[9], 'dp', scatter_dimension=0, tiled=True)  95.7 us
    all_gather x1, waiting for transfers between devices, shards(): lax.all_gather(inner_weight, 'dp', axis=1, tiled=True)  95.4 us
    all_gather x1, waiting for transfers between devices, shards(): lax.all_gather(outer_weight, 'dp', axis=1, tiled=True)  72.1 us
  transfers between devices with their start and end apart: 21, of which 20 were waited for; matrix products, arithmetic and copies ran while one was open for 9% of the time, Pallas kernels for 0%

commit v1 on v0

--- a/solution.py
+++ b/solution.py
@@ -7,6 +7,33 @@
 HEAD_DIM = 64
 SEG_LEN = 128
 epsilon = 1e-05
+
+
+def perform_tails_on_mesh(original, in_dim):
+    original = jnp.moveaxis(original, 0, in_dim)
+    low = original.shape
+    field_out = original.reshape(*low[:in_dim], low[in_dim] * low[in_dim + 1], *low[in_dim + 2 :])
+    return field_out
+
+
+def enter_sheets_on(t0, axis_id):
+    now = lax.axis_size(axis_id)
+    inter = lax.axis_index(axis_id)
+    local_out, piece_now = (now, inter)
+    local_next, known = (t0[None], 1)
+    while known < local_out:
+        y2 = lax.ppermute(local_next, axis_id, [(q, q ^ known) for q in range(local_out)])
+        ready = piece_now & known == 0
+        part_next = jnp.where(ready, local_next, y2)
+        res = jnp.where(ready, y2, local_next)
+        local_next = jnp.concatenate([part_next, res])
+        known *= 2
+    return local_next
+
+
+def _step_on_orders(u, state, dim_i):
+    seen_now = perform_tails_on_mesh(enter_sheets_on(u, state), dim_i)
+    return seen_now
 
 
 def normalize(values, gain, shift):
@@ -241,7 +268,7 @@
         lax.all_gather(key_weight, "dp", axis=1, tiled=True),
         lax.all_gather(value_weight, "dp", axis=1, tiled=True),
         lax.all_gather(out_weight, "dp", axis=1, tiled=True),
-        lax.all_gather(inner_weight, "dp", axis=1, tiled=True),
+        _step_on_orders(inner_weight, "dp", 1),
         lax.all_gather(outer_weight, "dp", axis=1, tiled=True),
     )
     stacked = (

time: 1630 us -> 1540 us (0.945)
  waiting for transfers between devices: 1260 us -> 1150 us
    all_gather x1 -> x0, waiting for transfers between devices: 95.4 us -> none  [shards(): lax.all_gather(inner_weight, 'dp', axis=1, tiled=True)]
    ppermute x0 -> x2, waiting for transfers between devices: none -> 74.3 us  [enter_sheets_on(): lax.ppermute(local_next, axis_id, [(q, q ^ known) for q in range(local_ou...]
    unnamed x31 -> x30, waiting for transfers between devices: 295 us -> 239 us
    all_gather x1, waiting for transfers between devices: 36 us -> 0.01 us  [shards(): lax.all_gather(query_weight, 'dp', axis=1, tiled=True)]
    all_gather x1, waiting for transfers between devices: 17.8 us -> 53.2 us  [shards(): lax.all_gather(value_weight, 'dp', axis=1, tiled=True)]
    all_gather x1, waiting for transfers between devices: 36.8 us -> 5.01 us  [shards(): lax.all_gather(key_weight, 'dp', axis=1, tiled=True)]
    unnamed x261 -> x251, local copies, waits for them, and re-layouts: 68.9 us -> 66.7 us
  transfers between devices with their start and end apart: 21 -> 22, of which waited for: 20 -> 17; matrix products, arithmetic and copies ran while one was open for 9% -> 15% of each run, Pallas kernels for 0% -> 0%
where the time goes in v1:
time: 1540 us
  waiting for transfers between devices  1150 us (75%)
  matrix products  142 us (9%)
  local copies, waits for them, and re-layouts  91.9 us (6%)
  other arithmetic  71.8 us (5%)
  blocking collectives  60 us (4%)
  between operations  17.4 us (1%)
    psum x1, waiting for transfers between devices, shards(): lax.psum((shares[0], shares[1], shares[2], shares[3], shares[4], shares[5...  282 us
    unnamed x30, waiting for transfers between devices  239 us
    reduce_scatter x1, waiting for transfers between devices, shards(): lax.psum_scatter(segment_grads[9], 'dp', scatter_dimension=0, tiled=True)  97.9 us
    reduce_scatter x1, waiting for transfers between devices, shards(): lax.psum_scatter(cross_grads[9], 'dp', scatter_dimension=0, tiled=True)  97.9 us
    reduce_scatter x1, waiting for transfers between devices, shards(): lax.psum_scatter(cross_grads[11], 'dp', scatter_dimension=0, tiled=True)  97.9 us
    reduce_scatter x1, waiting for transfers between devices, shards(): lax.psum_scatter(segment_grads[11], 'dp', scatter_dimension=0, tiled=True)  95.7 us
    ppermute x2, waiting for transfers between devices, enter_sheets_on(): lax.ppermute(local_next, axis_id, [(q, q ^ known) for q in range(local_ou...  74.3 us
    unnamed x251, local copies, waits for them, and re-layouts  66.7 us
  transfers between devices with their start and end apart: 22, of which 17 were waited for; matrix products, arithmetic and copies ran while one was open for 15% of the time, Pallas kernels for 0%

profile of v1, /device:TPU:0, one launch (start us, length us, event | category | flops | bytes accessed | tf_op | source)
XLA Modules:
  0.0 1535.9 jit_solution(6975883399805418757)
XLA Ops:
  10.1 3.0 collective-permute-start
  13.2 74.3 %collective-permute-done = bf16[1,2,192,3072]{3,2,1,0:T(8,128)(2,1)} collective-permute-done((bf16[1,2,192,3072]{3,2,1,0:T(8,128)(2,1)S(1)}, bf16[1,2,192,3072]{3,2,1,0:T(8,128)(2,1)}, u32[]{:S(2)}, u32[]{:S(2)}) %collective-permute-start) | collective-permute-done | bytes 2359328 | tf_op jit(solution)/shard_map/ppermute | solution.py:25
  95.4 14.3 all-gather.1
  114.2 2.9 add_convert_fusion.1
  119.4 5.0 all-gather.13.cloned.1.call-done
  124.4 2.9 convolution_convert_fusion.3
  129.6 53.2 %all-gather.9.cloned.1.call-done = bf16[2,768,768]{2,1,0:T(8,128)(2,1)} async-done(((bf16[2,192,768]{2,1,0:T(8,128)(2,1)}), bf16[2,768,768]{2,1,0:T(8,128)(2,1)}) %all-gather.9.cloned.1.call-update) | async-done | bytes 2359312 | tf_op jit(solution)/shard_map/all_gather | solution.py:269
  182.8 2.9 add_convert_fusion.2
  188.0 4.4 fusion.103
  192.4 3.7 convolution_convert_fusion.5
  196.1 44.6 %all-gather.15.cloned.1.call-done = bf16[2,768,768]{2,1,0:T(8,128)(2,1)} async-done(((bf16[2,192,768]{2,1,0:T(8,128)(2,1)}), bf16[2,768,768]{2,1,0:T(8,128)(2,1)}) %all-gather.15.cloned.1.call-update) | async-done | bytes 2359312 | tf_op jit(solution)/shard_map/all_gather | solution.py:270
  244.5 2.9 broadcast_select_fusion.1
  248.3 5.4 fusion.102
  253.8 7.8 fusion.28
  264.1 15.5 %multiply_convert_fusion = (bf16[4,128,3072]{2,1,0:T(8,128)(2,1)}, f32[4,128,3072]{2,1,0:T(8,128)}) fusion(f32[4,128,3072]{2,1,0:T(8,128)S(1)} %get-tuple-element.189, f32[3072]{0:T(1024)S(1)} %bitcast.350, u8[128,3072]{1,0:T(8,128)(4,1)S(1)} %get-tuple-element.73, u8[128,3072]{1,0:T(8,128)(4,1)S(1)} %get-tuple-element.72), kind=kLoop, calls=%fused_computation.20 | loop fusion | flops 111673344 | bytes 16527360 | tf_op jit(solution)/shard_map/convert_element_type | solution.py:120
  279.7 59.3 %all-gather.17.cloned.1.call-done = bf16[2,3072,768]{2,1,0:T(8,128)(2,1)} async-done(((bf16[2,768,768]{2,1,0:T(8,128)(2,1)}), bf16[2,3072,768]{2,1,0:T(8,128)(2,1)}) %all-gather.17.cloned.1.call-update) | async-done | bytes 9437200 | tf_op jit(solution)/shard_map/all_gather | solution.py:272
  339.0 6.0 fusion.105
  348.2 14.5 all-gather.2
  378.2 3.4 convolution_add_fusion
  381.7 3.9 fusion.41
  404.6 2.7 convolution_multiply_fusion.3
  429.3 9.9 convert_reduce_fusion
  439.3 3.6 multiply_reduce_fusion.2
  447.9 3.0 convolution_convert_fusion.2
  452.5 3.4 convert_reduce_fusion.3
  458.9 3.1 copy.176
  464.8 3.3 fusion.20
  473.0 3.0 copy.168
  481.7 3.1 copy.172
  486.1 8.2 convolution_bitcast_fusion
  495.3 5.8 convolution_multiply_fusion
  501.7 7.3 convolution_bitcast_fusion.1
  510.0 5.1 convolution_multiply_fusion.1
  532.4 24.3 %reduce-scatter.52.cloned.1.call-done = f32[192,768]{1,0:T(8,128)} async-done(((f32[768,768]{1,0:T(8,128)}), f32[192,768]{1,0:T(8,128)}) %reduce-scatter.52.cloned.1.call-update) | async-done | bytes 589840
  559.0 38.1 %reduce-scatter.48.cloned.1.call-done = f32[192,768]{1,0:T(8,128)} async-done(((f32[768,768]{1,0:T(8,128)}), f32[192,768]{1,0:T(8,128)}) %reduce-scatter.48.cloned.1.call-update) | async-done | bytes 589840
  599.3 38.8 %reduce-scatter.42.cloned.1.call-done = f32[192,768]{1,0:T(8,128)} async-done(((f32[768,768]{1,0:T(8,128)}), f32[192,768]{1,0:T(8,128)}) %reduce-scatter.42.cloned.1.call-update) | async-done | bytes 589840
  640.3 38.1 %reduce-scatter.40.cloned.1.call-done = f32[192,768]{1,0:T(8,128)} async-done(((f32[768,768]{1,0:T(8,128)}), f32[192,768]{1,0:T(8,128)}) %reduce-scatter.40.cloned.1.call-update) | async-done | bytes 589840
  680.6 38.2 %reduce-scatter.44.cloned.1.call-done = f32[192,768]{1,0:T(8,128)} async-done(((f32[768,768]{1,0:T(8,128)}), f32[192,768]{1,0:T(8,128)}) %reduce-scatter.44.cloned.1.call-update) | async-done | bytes 589840
  721.0 95.7 %reduce-scatter.36.cloned.1.call-done = f32[768,768]{1,0:T(8,128)} async-done(((f32[3072,768]{1,0:T(8,128)}), f32[768,768]{1,0:T(8,128)}) %reduce-scatter.36.cloned.1.call-update) | async-done | bytes 2359312 | tf_op jit(solution)/shard_map/reduce_scatter | solution.py:340
  816.7 97.9 %reduce-scatter.38.cloned.1.call-done = f32[768,768]{1,0:T(8,128)} async-done(((f32[3072,768]{1,0:T(8,128)}), f32[768,768]{1,0:T(8,128)}) %reduce-scatter.38.cloned.1.call-update) | async-done | bytes 2359312 | tf_op jit(solution)/shard_map/reduce_scatter | solution.py:355
  914.6 97.9 %reduce-scatter.32.cloned.1.call-done = f32[192,3072]{1,0:T(8,128)} async-done(((f32[768,3072]{1,0:T(8,128)}), f32[192,3072]{1,0:T(8,128)}) %reduce-scatter.32.cloned.1.call-update) | async-done | bytes 2359312 | tf_op jit(solution)/shard_map/reduce_scatter | solution.py:338
  1012.5 97.9 %reduce-scatter.34.cloned.1.call-done = f32[192,3072]{1,0:T(8,128)} async-done(((f32[768,3072]{1,0:T(8,128)}), f32[192,3072]{1,0:T(8,128)}) %reduce-scatter.34.cloned.1.call-update) | async-done | bytes 2359312 | tf_op jit(solution)/shard_map/reduce_scatter | solution.py:353
  1120.1 44.5 %all-reduce.26.cloned.1.call-done = (f32[768]{0:T(1024)}, f32[768]{0:T(1024)}, f32[768]{0:T(1024)}, f32[768]{0:T(1024)}, f32[768]{0:T(1024)}, /*index=5*/f32[768...) async-done(((f32[768]{0:T(1024)}, f32[768]{0:T(1024)}, ...) | async-done | bytes 73744
  1178.2 14.0 reduce-scatter.56.cloned.1.call-done
  1193.1 31.2 %all-reduce.18 = (f32[1,192]{1,0:T(1,128)S(1)}, f32[1,192]{1,0:T(1,128)S(1)}, f32[1,192]{1,0:T(1,128)S(1)}, f32[1,192]{1,0:T(1,128)S(1)}, f32[1,192]{1,0:T(1,128...) all-reduce(f32[1,192]{1,0:T(1,128)S(1)} %bitcast.354, ...), channel_id=1, replica_groups=mesh['dp'=4,'seg'=8] {'seg'}, use_global_device_ids=true, to_apply=%region_31.32 | all-reduce | flops 10752 | bytes 86016 | tf_op jit(solution)/shard_map/psum | solution.py:361
  1229.5 282.0 %all-reduce.24.cloned.1.call-done = (f32[1,192,768]{1,2,0:T(8,128)}, f32[1,192,768]{1,2,0:T(8,128)}, f32[1,192,768]{1,2,0:T(8,128)}, f32[1,192,768]{1,2,0:T(8,12...) async-done(((f32[1,192,768]{1,2,0:T(8,128)}, ...) | async-done | bytes 14155792 | tf_op jit(solution)/shard_map/psum | solution.py:361
  1520.8 5.0 pad_maximum_fusion.2
  1525.9 2.7 pad_maximum_fusion.1
  (430 shorter events, 181.0 us)
Async XLA Ops:
  7.2 107.0 %all-gather.11.cloned.1.call-start = ((), (), s32[]{:S(2)}) async-start(), calls=%async_computation.14 | async-start | bytes 2949120 | tf_op jit(solution)/shard_map/all_gather | solution.py:267
  7.9 116.5 %all-gather.13.cloned.1.call-start = ((), (), s32[]{:S(2)}) async-start(), calls=%async_computation.15 | async-start | bytes 2949120 | tf_op jit(solution)/shard_map/all_gather | solution.py:268
  8.7 174.1 %all-gather.9.cloned.1.call-start = ((), (), s32[]{:S(2)}) async-start(), calls=%async_computation.13 | async-start | bytes 2949120 | tf_op jit(solution)/shard_map/all_gather | solution.py:269
  9.4 231.3 %all-gather.15.cloned.1.call-start = ((), (), s32[]{:S(2)}) async-start(), calls=%async_computation.16 | async-start | bytes 2949120 | tf_op jit(solution)/shard_map/all_gather | solution.py:270
  10.0 328.9 %all-gather.17.cloned.1.call-start = ((), (), s32[]{:S(2)}) async-start(), calls=%async_computation.17 | async-start | bytes 11796480 | tf_op jit(solution)/shard_map/all_gather | solution.py:272
  10.1 77.4 %collective-permute-start = (bf16[1,2,192,3072]{3,2,1,0:T(8,128)(2,1)S(1)}, bf16[1,2,192,3072]{3,2,1,0:T(8,128)(2,1)}, u32[]{:S(2)}, u32[]{:S(2)}) collective-permute-start(bf16[1,2,192,3072]{3,2,1,0:T(8,128)(2,1)S(1)} %bitcast.336), channel_id=1, source_target_pairs={{0,8},{8,0},{16,24},{24,16},{1,9},{9,1},{17,25},{25,17},{2,10},{10... | collective-permute-start | bytes 7077896 | tf_op jit(solution)/shard_map/ppermute | solution.py:25
  13.1 512.6 %reduce-scatter.54.cloned.1.call-start = ((), (), s32[]{:S(2)}) async-start(), calls=%async_computation.29 | async-start | bytes 2949120
  90.2 19.6 %copy-start.80 = (bf16[2,768]{1,0:T(2,128)(2,1)S(1)}, bf16[2,768]{1,0:T(2,128)(2,1)}, u32[]{:S(2)}) copy-start(bf16[2,768]{1,0:T(2,128)(2,1)} %param.23) | copy-start | bytes 9220
  90.2 19.6 %copy-start.81 = (bf16[2,768]{1,0:T(2,128)(2,1)S(1)}, bf16[2,768]{1,0:T(2,128)(2,1)}, u32[]{:S(2)}) copy-start(bf16[2,768]{1,0:T(2,128)(2,1)} %param.26) | copy-start | bytes 9220
  90.2 20.2 %copy-start.82 = (bf16[2,768]{1,0:T(2,128)(2,1)S(1)}, bf16[2,768]{1,0:T(2,128)(2,1)}, u32[]{:S(2)}) copy-start(bf16[2,768]{1,0:T(2,128)(2,1)} %param.28) | copy-start | bytes 9220
  90.2 20.8 %copy-start.83 = (bf16[2,768]{1,0:T(2,128)(2,1)S(1)}, bf16[2,768]{1,0:T(2,128)(2,1)}, u32[]{:S(2)}) copy-start(bf16[2,768]{1,0:T(2,128)(2,1)} %param.29) | copy-start | bytes 9220
  90.2 21.4 %copy-start.84 = (bf16[2,768]{1,0:T(2,128)(2,1)S(1)}, bf16[2,768]{1,0:T(2,128)(2,1)}, u32[]{:S(2)}) copy-start(bf16[2,768]{1,0:T(2,128)(2,1)} %param.34) | copy-start | bytes 9220
  90.2 21.4 %copy-start.85 = (bf16[2,768]{1,0:T(2,128)(2,1)S(1)}, bf16[2,768]{1,0:T(2,128)(2,1)}, u32[]{:S(2)}) copy-start(bf16[2,768]{1,0:T(2,128)(2,1)} %param.30) | copy-start | bytes 9220
  90.2 22.0 %copy-start.86 = (bf16[2,768]{1,0:T(2,128)(2,1)S(1)}, bf16[2,768]{1,0:T(2,128)(2,1)}, u32[]{:S(2)}) copy-start(bf16[2,768]{1,0:T(2,128)(2,1)} %param.36) | copy-start | bytes 9220
  90.2 22.0 %copy-start.87 = (bf16[2,768]{1,0:T(2,128)(2,1)S(1)}, bf16[2,768]{1,0:T(2,128)(2,1)}, u32[]{:S(2)}) copy-start(bf16[2,768]{1,0:T(2,128)(2,1)} %param.35) | copy-start | bytes 9220
  90.3 22.6 %copy-start.96 = (s32[1,32]{1,0:T(1,128)S(1)}, s32[1,32]{1,0:T(1,128)}, u32[]{:S(2)}) copy-start(s32[1,32]{1,0:T(1,128)} %param.20) | copy-start | bytes 388
  90.3 23.3 %copy-start.63 = (bf16[2,3072]{1,0:T(2,128)(2,1)S(1)}, bf16[2,3072]{1,0:T(2,128)(2,1)}, u32[]{:S(2)}) copy-start(bf16[2,3072]{1,0:T(2,128)(2,1)} %param.32) | copy-start | bytes 36868
  90.3 23.9 %copy-start.7 = (bf16[1,512,768]{2,1,0:T(8,128)(2,1)S(1)}, bf16[1,512,768]{2,1,0:T(8,128)(2,1)}, u32[]{:S(2)}) copy-start(bf16[1,512,768]{2,1,0:T(8,128)(2,1)} %param.19) | copy-start | bytes 2359300
  93.1 151.4 %collective-permute-start.1 = (bf16[2,2,192,3072]{3,2,1,0:T(8,128)(2,1)}, bf16[2,2,192,3072]{3,2,1,0:T(8,128)(2,1)}, u32[]{:S(2)}, u32[]{:S(2)}) collective-permute-start(bf16[2,2,192,3072]{3,2,1,0:T(8,128)(2,1)} %pad_maximum_fusion), channel_id=1, source_target_pairs={{0,16},{8,24},{16,0},{24,8},{1,17},{9,25},{17,1},{25,9},{2,18},{10... | collective-permute-start | bytes 14155784 | tf_op jit(solution)/shard_map/ppermute | solution.py:25
  111.6 227.3 %copy-start.78 = (f32[768]{0:T(1024)}, f32[768]{0:T(1024)S(1)}, u32[]{:S(2)}) copy-start(f32[768]{0:T(1024)S(1)} %get-tuple-element.91) | copy-start | bytes 9220
  112.2 226.7 %copy-start.93 = (f32[768]{0:T(1024)}, f32[768]{0:T(1024)S(1)}, u32[]{:S(2)}) copy-start(f32[768]{0:T(1024)S(1)} %get-tuple-element.213) | copy-start | bytes 9220
  112.9 233.0 %copy-start.55 = (f32[768]{0:T(1024)}, f32[768]{0:T(1024)S(1)}, u32[]{:S(2)}) copy-start(f32[768]{0:T(1024)S(1)} %get-tuple-element.215) | copy-start | bytes 9220
  114.2 147.4 %copy-start.61 = (f32[1,3072]{1,0:T(1,128)}, f32[1,3072]{1,0:T(1,128)S(1)}, u32[]{:S(2)}) copy-start(f32[1,3072]{1,0:T(1,128)S(1)} %get-tuple-element.184) | copy-start | bytes 36868
  243.3 95.7 %copy-start.68 = (f32[4,128]{1,0:T(4,128)}, f32[4,128]{1,0:T(4,128)S(1)}, u32[]{:S(2)}) copy-start(f32[4,128]{1,0:T(4,128)S(1)} %broadcast_multiply_fusion.11) | copy-start | bytes 6148
  244.5 94.5 %copy-start.90 = (f32[4,128]{1,0:T(4,128)}, f32[4,128]{1,0:T(4,128)S(1)}, u32[]{:S(2)}) copy-start(f32[4,128]{1,0:T(4,128)S(1)} %fusion.91) | copy-start | bytes 6148
  264.1 74.8 %copy-start.3 = (f32[4,128,768]{2,1,0:T(8,128)S(1)}, f32[4,128,768]{2,1,0:T(8,128)}, u32[]{:S(2)}) copy-start(f32[4,128,768]{2,1,0:T(8,128)} %copy-done.2) | copy-start | bytes 4718596
  364.4 9.3 copy-start.42
  378.2 10.7 slice-start.4
  397.8 130.1 %reduce-scatter.50.cloned.1.call-start = ((), (), s32[]{:S(2)}) async-start(), calls=%async_computation.27 | async-start | bytes 2949120
  407.3 122.9 %reduce-scatter.46.cloned.1.call-start = ((), (), s32[]{:S(2)}) async-start(), calls=%async_computation.25 | async-start | bytes 2949120
  426.3 130.5 %reduce-scatter.52.cloned.1.call-start = ((), (), s32[]{:S(2)}) async-start(), calls=%async_computation.28 | async-start | bytes 2949120
  428.4 10.8 slice-start.2
  429.3 10.0 copy-start.35
  429.3 10.0 slice-start.3
  429.3 10.0 copy-start.69
  429.3 10.0 copy-start.79
  429.3 10.0 copy-start.91
  447.7 149.4 %reduce-scatter.48.cloned.1.call-start = ((), (), s32[]{:S(2)}) async-start(), calls=%async_computation.26 | async-start | bytes 2949120
  462.1 176.0 %reduce-scatter.42.cloned.1.call-start = ((), (), s32[]{:S(2)}) async-start(), calls=%async_computation.23 | async-start | bytes 2949120
  464.7 213.6 %reduce-scatter.40.cloned.1.call-start = ((), (), s32[]{:S(2)}) async-start(), calls=%async_computation.22 | async-start | bytes 2949120
  476.1 242.7 %reduce-scatter.44.cloned.1.call-start = ((), (), s32[]{:S(2)}) async-start(), calls=%async_computation.24 | async-start | bytes 2949120
  484.8 331.9 %reduce-scatter.36.cloned.1.call-start = ((), (), s32[]{:S(2)}) async-start(), calls=%async_computation.20 | async-start | bytes 11796480 | tf_op jit(solution)/shard_map/reduce_scatter | solution.py:340
  494.3 420.3 %reduce-scatter.38.cloned.1.call-start = ((), (), s32[]{:S(2)}) async-start(), calls=%async_computation.21 | async-start | bytes 11796480 | tf_op jit(solution)/shard_map/reduce_scatter | solution.py:355
  501.1 511.4 %reduce-scatter.32.cloned.1.call-start = ((), (), s32[]{:S(2)}) async-start(), calls=%async_computation.18 | async-start | bytes 11796480 | tf_op jit(solution)/shard_map/reduce_scatter | solution.py:338
  509.0 601.3 %reduce-scatter.34.cloned.1.call-start = ((), (), s32[]{:S(2)}) async-start(), calls=%async_computation.19 | async-start | bytes 11796480 | tf_op jit(solution)/shard_map/reduce_scatter | solution.py:353
  515.1 649.5 %all-reduce.26.cloned.1.call-start = ((), (), s32[]{:S(2)}) async-start(), calls=%async_computation.32 | async-start | bytes 180224
  524.6 667.6 %reduce-scatter.56.cloned.1.call-start = ((), (), s32[]{:S(2)}) async-start(), calls=%async_computation.30 | async-start | bytes 491520
  525.6 985.9 %all-reduce.24.cloned.1.call-start = ((), (), s32[]{:S(2)}) async-start(), calls=%async_computation.31 | async-start | bytes 31457280 | tf_op jit(solution)/shard_map/psum | solution.py:361
  (81 other events, 256.5 us)
Sparse Core Ops, SparseCore 0:
  9.8 58.9 all-gather.10
  70.7 53.6 all-gather.12
  126.2 56.4 all-gather.8
  184.5 56.1 all-gather.14
  242.4 96.5 all-gather.16
  398.0 37.3 reduce-scatter.53
  438.4 37.3 reduce-scatter.49
  478.8 37.3 reduce-scatter.45
  519.3 37.3 reduce-scatter.51
  559.6 37.3 reduce-scatter.47
  600.7 37.3 reduce-scatter.41
  641.0 37.3 reduce-scatter.39
  681.4 37.3 reduce-scatter.43
  721.8 94.8 reduce-scatter.35
  819.7 94.8 reduce-scatter.37
  917.5 94.8 reduce-scatter.31
  1015.4 94.8 reduce-scatter.33
  1116.1 48.4 all-reduce.25
  1167.4 24.6 reduce-scatter.55
  1196.6 314.9 all-reduce.23
